TPU v7x, 512 devices: a whole 4x8x8 slice. The times are simulated.
512 devices in a mesh: vocab: 64 (over y, x, core), width: 8 (over z).
Axes of the slice: x: 4, y: 8, z: 8, core: 2. Of those that a mesh axis runs over, the one named last changes fastest.
Arguments:
- hidden: bfloat16 [8192, 2048], P('vocab', 'width'), may hold values from -400 to 400
- norm_gain: bfloat16 [2048], P('width'), may hold values from 0.5 to 1.5
- head_weight: bfloat16 [102400, 2048], P('vocab', 'width'), may hold values from -1 to 1
- targets: int32 [8192], P(('vocab', 'width')), may hold values from 0 to 102399
- pad_mask: int32 [8192], P(('vocab', 'width')), may hold values 0 or 1
- lengths: int32 [64], replicated, may hold values from 1 to 2048, 8192 in all
Outputs:
- entropy: float32 [8192], P(('vocab', 'width'))
- token_logprob: float32 [8192], P(('vocab', 'width'))
- seq_score: float32 [64], replicated
Inputs may be any that keep to these rules, and one draw needn't show every extreme that they name: The lengths sum to 8192.
All inputs are finite; a program needn't handle non-finite values. No bound on the sum of `pad_mask` on one device may be relied on, other than what follows from the above.
Results may differ from a plain program's by a relative error of at most 0.0031.
Values may be sent and summed in bfloat16 or wider, within the bound.
A program may use at most 64 MiB of HBM per device.

v0:
```python
import math

import jax
import jax.numpy as jnp
from jax import lax
from jax.sharding import PartitionSpec as P

epsilon = 1e-06


def merged_2(value, axis, join):
    pieces = jax.tree.map(lambda part: lax.all_gather(part, axis), value)
    head = jax.tree.map(lambda part: part[0], pieces)
    tail = jax.tree.map(lambda part: part[1:], pieces)
    total, _ = lax.scan(lambda total, piece: (join(total, piece), None), head, tail)
    return total


def summarize(logits, block_ids, first_col):
    peak = jnp.max(logits, axis=1)
    shifted = logits - peak[:, None]
    weights = jnp.exp(shifted)
    exp_total = jnp.sum(weights, axis=1)
    spread = jnp.sum(weights * shifted, axis=1)
    columns = first_col + lax.iota(jnp.int32, logits.shape[1])
    target_logit = jnp.sum(jnp.where(columns[None, :] == block_ids[:, None], logits, 0.0), axis=1)
    return (peak, exp_total, spread, target_logit)


def combine(earlier, later):
    peak = jnp.maximum(earlier[0], later[0])
    left_lift = jnp.exp(earlier[0] - peak)
    right_lift = jnp.exp(later[0] - peak)
    exp_total = earlier[1] * left_lift + later[1] * right_lift
    spread = left_lift * (earlier[2] + (earlier[0] - peak) * earlier[1]) + right_lift * (
        later[2] + (later[0] - peak) * later[1]
    )
    return (peak, exp_total, spread, earlier[3] + later[3])


def per_device(hidden, norm_gain, head_weight, targets, pad_mask, lengths):
    width_count = lax.axis_size("width")
    own_count = targets.shape[0]
    values = hidden.astype(jnp.float32)
    energy = lax.psum(jnp.sum(values * values, axis=1), "width")
    inv_rms = lax.rsqrt(energy / (hidden.shape[1] * width_count) + epsilon)
    normed = (values * inv_rms[:, None] * norm_gain.astype(jnp.float32)[None, :]).astype(
        jnp.bfloat16
    )
    full_rows = lax.all_to_all(normed, "width", split_axis=0, concat_axis=1, tiled=True)
    gathered, gathered_ids = (
        lax.all_gather(full_rows, "vocab", axis=0, tiled=True),
        lax.all_gather(targets, "vocab", axis=0, tiled=True),
    )
    col_count = head_weight.shape[0]
    first_col = lax.axis_index("vocab") * col_count
    total_rows = gathered.shape[0]
    block_rows = math.gcd(total_rows, 512)
    contract = (((1,), (1,)), ((), ()))
    head_full = lax.all_gather(head_weight, "width", axis=1, tiled=True)

    def per_block(inputs):
        logits = lax.dot_general(inputs[0], head_full, contract, preferred_element_type=jnp.float32)
        return summarize(logits, inputs[1], first_col)

    blocked = lax.map(
        per_block,
        (gathered.reshape(-1, block_rows, gathered.shape[1]), gathered_ids.reshape(-1, block_rows)),
    )
    statistics = (
        blocked[0].reshape(-1),
        blocked[1].reshape(-1),
        blocked[2].reshape(-1),
        blocked[3].reshape(-1),
    )
    merged = merged_2(statistics, "vocab", combine)
    own_start = lax.axis_index("vocab") * own_count
    peak = lax.dynamic_slice_in_dim(merged[0], own_start, own_count, 0)
    exp_total = lax.dynamic_slice_in_dim(merged[1], own_start, own_count, 0)
    spread = lax.dynamic_slice_in_dim(merged[2], own_start, own_count, 0)
    target_logit = lax.dynamic_slice_in_dim(merged[3], own_start, own_count, 0)
    kept_mask = pad_mask.astype(jnp.float32)
    log_total = jnp.log(exp_total)
    entropy = kept_mask * (log_total - spread / exp_total)
    token_logprob = kept_mask * (target_logit - peak - log_total)
    device_index = lax.axis_index("vocab") * width_count + lax.axis_index("width")
    token_index = device_index * own_count + lax.iota(jnp.int32, own_count)
    seq_ends = jnp.cumsum(lengths)
    seq_starts = seq_ends - lengths
    member = (
        (token_index[:, None] >= seq_starts[None, :]) & (token_index[:, None] < seq_ends[None, :])
    ).astype(jnp.float32)
    partial_value = jnp.sum(member * token_logprob[:, None], axis=0)
    seq_score = lax.psum(partial_value, ("vocab", "width")) / lengths.astype(jnp.float32)
    return (entropy, token_logprob, seq_score)


def solution(mesh):
    placed = (
        P("vocab", "width"),
        P("width"),
        P("vocab", "width"),
        P(("vocab", "width")),
        P(("vocab", "width")),
        P(),
    )
    return jax.shard_map(
        per_device,
        mesh=mesh,
        in_specs=placed,
        out_specs=(P(("vocab", "width")), P(("vocab", "width")), P()),
        check_vma=False,
    )
```

profile of v0, /device:TPU:1, one launch (start us, length us, event | category | flops | bytes accessed | tf_op | source)
XLA Modules:
  0.0 491.1 jit_solution(4575408305845917003)
XLA Ops:
  7.2 0.0 all-gather.7.cloned.1.call-start
  7.2 0.9 fusion.5
  8.2 20.3 %psum.14 = f32[128]{0:T(128)S(1)} all-reduce(f32[128]{0:T(128)S(1)} %fusion.5), channel_id=1, replica_groups=mesh['vocab'=64,'width'=8] {'width'}, use_global_device_ids=true, to_apply=%region_1.0 | all-reduce | flops 128 | bytes 1024 | tf_op jit(solution)/shard_map/psum | solution.py:45
  28.4 0.7 convert_element_type.18
  29.1 0.9 fusion.7
  30.0 9.6 %all_to_all.19 = bf16[8,16,256]{2,1,0:T(8,128)(2,1)S(1)} all-to-all(bf16[8,16,256]{2,1,0:T(8,128)(2,1)S(1)} %bitcast.73), channel_id=1, replica_groups=mesh['vocab'=64,'width'=8] {'width'}, dimensions={0} | all-to-all | bytes 131072 | tf_op jit(solution)/shard_map/all_to_all | solution.py:50
  39.6 0.6 copy.21
  40.2 0.0 all-gather.7.cloned.1.call-update
  40.3 0.0 all-gather.9.cloned.1.call-start
  40.3 0.7 all-gather.9.cloned.1.call-update
  41.1 1.3 dynamic-slice
  43.0 0.9 dynamic-update-slice
  43.9 22.5 %all-reduce = s32[1024]{0:T(1024)S(1)} all-reduce(s32[1024]{0:T(1024)S(1)} %dynamic-update-slice), channel_id=1, replica_groups=mesh['vocab'=64,'width'=8] {'vocab'}, use_global_device_ids=true, to_apply=%add | all-reduce | flops 1024 | bytes 8192
  66.4 0.7 copy.16
  67.2 0.1 reduce-window.8
  67.3 0.1 reduce
  67.4 0.7 sub.31
  68.0 58.4 %all-gather.7.cloned.1.call-done = bf16[1024,2048]{1,0:T(8,128)(2,1)} async-done(((bf16[16,2048]{1,0:T(8,128)(2,1)}), bf16[1024,2048]{1,0:T(8,128)(2,1)}) %all-gather.7.cloned.1.call-update) | async-done | bytes 4194320 | tf_op jit(solution)/shard_map/all_gather | solution.py:52
  126.4 83.2 %all-gather.9.cloned.1.call-done = bf16[1600,2048]{1,0:T(8,128)(2,1)} async-done(((bf16[1600,256]{1,0:T(8,128)(2,1)}), bf16[1600,2048]{1,0:T(8,128)(2,1)}) %all-gather.9.cloned.1.call-update) | async-done | bytes 6553616 | tf_op jit(solution)/shard_map/all_gather | solution.py:60
  209.6 16.2 %while.32 = (s32[]{:T(128)}, f32[2,512]{1,0:T(2,128)S(1)}, f32[2,512]{1,0:T(2,128)S(1)}, f32[2,512]{1,0:T(2,128)S(1)}, f32[2,512]{1,0:T(2,128)S(1)}, /*index=5*/...) while((s32[]{:T(128)}, f32[2,512]{1,0:T(2,128)S(1)}, ...), condition=%wide.region_7.8_spmd, body=%wide.region_2.7_spmd.sunk | while | flops 3361996288 | bytes 15250565 | solution.py:66
  209.6 6.4 %fusion.14 = (f32[512]{0:T(512)S(1)}, f32[512,1600]{0,1:T(8,128)S(1)}) fusion(bf16[1600,2048]{1,0:T(8,128)(2,1)} %get-tuple-element.320, bf16[2,512,2048]{2,1,0:T(8,128)(2,1)} %get-tuple-element.319, s32[]{:T(128)} %get-tuple-element.303), kind=kOutput, calls=%fused_computation.31.clone.1 | convolution fusion | flops 3356261888 | bytes 11930112 | tf_op jit(solution)/shard_map/while/body/eval_jaxpr/dot_general | solution.py:63
  216.1 1.4 fusion.15
  217.7 6.4 %fusion.14 = (f32[512]{0:T(512)S(1)}, f32[512,1600]{0,1:T(8,128)S(1)}) fusion(bf16[1600,2048]{1,0:T(8,128)(2,1)} %get-tuple-element.320, bf16[2,512,2048]{2,1,0:T(8,128)(2,1)} %get-tuple-element.319, s32[]{:T(128)} %get-tuple-element.303), kind=kOutput, calls=%fused_computation.31.clone.1 | convolution fusion | flops 3356261888 | bytes 11930112 | tf_op jit(solution)/shard_map/while/body/eval_jaxpr/dot_general | solution.py:63
  224.2 1.4 fusion.15
  225.8 0.0 copy-start.2
  225.8 0.0 copy-start.1
  225.8 42.7 %all-gather = f32[64,1,1024]{2,1,0:T(1,128)S(1)} all-gather(f32[1,1,1024]{2,1,0:T(1,128)S(1)} %reshape.60), channel_id=1, replica_groups=mesh['vocab'=64,'width'=8] {'vocab'}, dimensions={0}, use_global_device_ids=true | all-gather | bytes 266240 | tf_op jit(solution)/shard_map/all_gather | solution.py:12
  268.6 37.2 %all-gather.1 = f32[64,1,1024]{2,1,0:T(1,128)S(1)} all-gather(f32[1,1,1024]{2,1,0:T(1,128)S(1)} %reshape.62), channel_id=1, replica_groups=mesh['vocab'=64,'width'=8] {'vocab'}, dimensions={0}, use_global_device_ids=true | all-gather | bytes 266240 | tf_op jit(solution)/shard_map/all_gather | solution.py:12
  305.8 36.9 %all-gather.2 = f32[64,1,1024]{2,1,0:T(1,128)S(1)} all-gather(f32[1,1,1024]{2,1,0:T(1,128)S(1)} %reshape.64), channel_id=1, replica_groups=mesh['vocab'=64,'width'=8] {'vocab'}, dimensions={0}, use_global_device_ids=true | all-gather | bytes 266240 | tf_op jit(solution)/shard_map/all_gather | solution.py:12
  342.7 37.1 %all-gather.3 = f32[64,1,1024]{2,1,0:T(1,128)S(1)} all-gather(f32[1,1,1024]{2,1,0:T(1,128)S(1)} %reshape.66), channel_id=1, replica_groups=mesh['vocab'=64,'width'=8] {'vocab'}, dimensions={0}, use_global_device_ids=true | all-gather | bytes 266240 | tf_op jit(solution)/shard_map/all_gather | solution.py:12
  380.2 7.6 %while.33 = (s32[]{:T(128)}, f32[1024]{0:T(1024)S(1)}, f32[1024]{0:T(1024)S(1)}, f32[1024]{0:T(1024)S(1)}, f32[1024]{0:T(1024)S(1)}, /*index=5*/f32[63,1024]{1,0...) while((s32[]{:T(128)}, f32[1024]{0:T(1024)S(1)}, ...), condition=%wide.region_9.10_spmd, body=%wide.region_8.9_spmd.sunk | while | flops 16386 | bytes 110701 | solution.py:15
  387.7 0.0 copy-done.2
  387.7 0.6 subtract_multiply_fusion
  388.3 0.0 copy-start
  388.3 0.1 select_reduce_fusion.1
  388.4 95.3 %psum.15 = f32[64]{0:T(128)S(1)} all-reduce(f32[64]{0:T(128)S(1)} %select_reduce_fusion.1), channel_id=1, replica_groups=mesh['vocab'=64,'width'=8] {'vocab','width'}, use_global_device_ids=true, to_apply=%region_12.13 | all-reduce | flops 64 | bytes 512 | tf_op jit(solution)/shard_map/psum | solution.py:94
  483.7 0.0 copy-done.1
  483.7 0.5 convert_divide_fusion
  484.2 0.0 copy-done
  (414 shorter events, 4.6 us)
Async XLA Ops:
  7.2 119.3 %all-gather.7.cloned.1.call-start = ((), (), s32[]{:S(2)}) async-start(), calls=%async_computation.1 | async-start | bytes 4259840 | tf_op jit(solution)/shard_map/all_gather | solution.py:52
  40.3 169.3 %all-gather.9.cloned.1.call-start = ((), (), s32[]{:S(2)}) async-start(), calls=%async_computation.2 | async-start | bytes 7372800 | tf_op jit(solution)/shard_map/all_gather | solution.py:60
  225.8 162.0 %copy-start.2 = (s32[16]{0:T(128)S(1)}, s32[16]{0:T(128)}, u32[]{:S(2)}) copy-start(s32[16]{0:T(128)} %param.14) | copy-start | bytes 196
  225.8 257.9 %copy-start.1 = (s32[64]{0:T(128)S(1)}, s32[64]{0:T(128)}, u32[]{:S(2)}) copy-start(s32[64]{0:T(128)} %param.15) | copy-start | bytes 772
  388.3 95.9 %copy-start = (f32[16]{0:T(128)}, f32[16]{0:T(128)S(1)}, u32[]{:S(2)}) copy-start(f32[16]{0:T(128)S(1)} %get-tuple-element.158) | copy-start | bytes 196
Sparse Core Ops, SparseCore 0:
  40.4 85.9 all-gather.6
  128.4 81.1 all-gather.8
where the time goes:
time: 491 us
  blocking collectives  302 us (62%)
  waiting for transfers between devices  142 us (29%)
  between operations  14.9 us (3%)
  matrix products  12.9 us (3%)
  other arithmetic  9.19 us (2%)
  local copies, waits for them, and re-layouts  6.36 us (1%)
    all_gather x4, blocking collectives, merged_2(): pieces = jax.tree.map(lambda part: lax.all_gather(part, axis), value)  154 us
    psum x1, blocking collectives, per_device(): lax.psum(partial_value, ('vocab', 'width')) / lengths.astype(jnp.float32)  95.3 us
    all_gather x1, waiting for transfers between devices, per_device(): head_full = lax.all_gather(head_weight, 'width', axis=1, tiled=True)  83.2 us
    all_gather x1, waiting for transfers between devices, per_device(): lax.all_gather(full_rows, 'vocab', axis=0, tiled=True)  58.4 us
    unnamed x1, blocking collectives  22.5 us
    psum x1, blocking collectives, per_device(): energy = lax.psum(jnp.sum(values * values, axis=1), 'width')  20.3 us
    dot_general x2, matrix products, per_block(): lax.dot_general(inputs[0], head_full, contract, preferred_element_type=jn...  12.9 us
  transfers between devices with their start and end apart: 2, of which 2 were waited for; matrix products, arithmetic and copies ran while one was open for 1% of the time, Pallas kernels for 0%

commit v1 on v0

v1 whole, which is shorter than its diff:
```python
import functools

import jax
import jax.numpy as jnp
from jax import lax
from jax.experimental import pallas as pl
from jax.experimental.pallas import tpu as pltpu
from jax.sharding import PartitionSpec as P

epsilon = 1e-06
MESH = pl.DeviceIdType.MESH
NX, NY, NC, NZ = 4, 8, 2, 8
GROUP = NC * NX
F32 = jnp.float32
NT = (((1,), (1,)), ((), ()))


def remote(src, dst, send, recv, device):
    return pltpu.make_async_remote_copy(
        src_ref=src, dst_ref=dst, send_sem=send, recv_sem=recv, device_id=device, device_id_type=MESH
    )


def merge_tiles(tiles):
    peak = functools.reduce(jnp.maximum, [t[0:1] for t in tiles])
    total = spread = target = None
    for t in tiles:
        gap = t[0:1] - peak
        lift = jnp.exp(gap)
        parts = (t[1:2] * lift, lift * (t[2:3] + gap * t[1:2]), t[3:4])
        if total is None:
            total, spread, target = parts
        else:
            total, spread, target = total + parts[0], spread + parts[1], target + parts[2]
    return peak, total, spread, target


def stack_rows(*rows):
    return jnp.concatenate(rows + (jnp.zeros((8 - len(rows), rows[0].shape[1]), F32),), axis=0)


def kernel(
    packed, digits, head, bounds, final, seq,
    raw, toks, heads, acc, stats, got_y, got_c, sum_z, sum_y,
    az_s, az_r, h_s, h_r, x_s, x_r, y_s, y_r, c_s, c_r, t_s, t_r,
):
    v = lax.axis_index("vocab")
    w = lax.axis_index("width")
    core = v % NC
    x = (v // NC) % NX
    y = v // (NC * NX)
    mine = core * NX + x
    rows, wide = head.shape
    ways, parts = 2, 2
    piece = rows // (ways * parts)

    def at_z(d):
        return {"width": (w + d) % NZ}

    def at_y(d):
        return {"vocab": (((y + d) % NY) * NX + x) * NC + core}

    def at_c(d):
        other = (mine + d) % GROUP
        return {"vocab": (y * NX + other % NX) * NC + other // NX}

    def at_x(d):
        return {"vocab": (y * NX + (x + d) % NX) * NC + core}

    barrier = pltpu.get_barrier_semaphore()
    for d in range(1, 8):
        for device in (at_z(d), at_y(d), at_c(d)):
            pl.semaphore_signal(barrier, inc=1, device_id=device, device_id_type=MESH)
    pl.semaphore_wait(barrier, 21)

    sent = []
    for d in range(1, NZ):
        copy = remote(packed.at[(w + d) % NZ], raw.at[w], az_s.at[d - 1], az_r.at[d - 1], at_z(d))
        copy.start()
        sent.append(copy)

    def head_copy(step, way, part):
        span = pl.ds((way * parts + part) * piece, piece)
        owner = (w - step + NZ) % NZ if way == 0 else (w + step) % NZ
        src = head.at[span] if step == 0 else heads.at[owner, span]
        return remote(
            src, heads.at[owner, span], h_s.at[way, step, part], h_r.at[way, step, part],
            at_z(1 if way == 0 else NZ - 1),
        )

    ring = {}

    def head_step(step):
        for part in range(parts):
            for way in range(ways):
                if step > 0:
                    ring[step - 1, way, part].wait_recv()
                if step < NZ - 1:
                    copy = head_copy(step, way, part)
                    copy.start()
                    ring[step, way, part] = copy

    head_step(0)
    raw[w] = packed[w]
    acc[...] = jnp.zeros_like(acc)
    for copy in sent:
        copy.wait_recv()

    values = raw[:, 0:16, :].astype(F32)
    gain = raw[:, 16:32, :].astype(F32)
    energy = jnp.sum(jnp.sum(values * values, axis=0), axis=1, keepdims=True)
    inv = lax.rsqrt(energy / (wide * NZ) + epsilon)
    toks[y, mine, 0:NZ] = (values * inv[None] * gain).astype(jnp.bfloat16)
    toks[y, mine, NZ] = digits[...]

    spot = toks.at[y, mine]
    xs = []
    for d in range(1, NX):
        copy = remote(spot, spot, x_s.at[d - 1], x_r.at[d - 1], at_x(d))
        copy.start()
        xs.append(copy)
    for copy in xs:
        copy.wait_recv()

    yring = {}

    def y_step(step):
        for way, hops in ((0, NY // 2), (1, NY // 2 - 1)):
            if 0 < step <= hops:
                yring[step - 1, way].wait_recv()
            if step < hops:
                owner = (y - step + NY) % NY if way == 0 else (y + step) % NY
                block = toks.at[owner, pl.ds(core * NX, NX)]
                copy = remote(
                    block, block, y_s.at[way, step], y_r.at[way, step], at_y(1 if way == 0 else NY - 1)
                )
                copy.start()
                yring[step, way] = copy

    y_step(0)
    for step in range(1, NY // 2 + 1):
        head_step(step)
        y_step(step)
    side = toks.at[:, pl.ds(core * NX, NX)]
    cross = remote(side, side, c_s.at[0], c_r.at[0], {"vocab": v - core + (1 - core)})
    cross.start()

    half = rows // ways

    def multiply(near, far):
        def one(i, carry):
            step = near + i // 4
            tile = i % 4
            lanes = pl.ds(pl.multiple_of(tile * 256, 256), 256)
            for way in range(ways):
                owner = (w - step + NZ) % NZ if way == 0 else (w + step) % NZ
                tokens = toks[pl.ds(tile * 2, 2), :, owner].reshape(256, wide)
                block = heads[owner, pl.ds(way * half, half)]
                span = pl.ds(way * half, half)
                acc[span, lanes] += lax.dot_general(block, tokens, NT, preferred_element_type=F32)
            return carry

        lax.fori_loop(0, (far - near) * 4, one, 0)

    heads[w] = head[...]
    head_step(5)
    cross.wait_recv()
    multiply(0, 3)
    head_step(6)
    multiply(3, 7)
    head_step(7)
    multiply(7, 8)

    chunk = rows // 10
    pick = (
        lax.broadcasted_iota(jnp.int32, (8, 256), 0) == lax.broadcasted_iota(jnp.int32, (8, 256), 1)
    ).astype(jnp.bfloat16)

    def side_values(block):
        return lax.dot_general(pick, block.reshape(128, 256), NT, preferred_element_type=F32)

    def fold(values, op):
        return op(values.reshape(chunk // 8, 8, 128), axis=0)

    def summarize(tile, carry):
        lanes = pl.ds(pl.multiple_of(tile * 128, 128), 128)
        extra = side_values(toks[tile, :, NZ])
        wanted = extra[0:1] * 4096.0 + extra[1:2] * 64.0 + extra[2:3] - (v * rows).astype(F32)
        wanted = wanted.astype(jnp.int32)

        def top(i, peak):
            return jnp.maximum(peak, fold(acc[pl.ds(i * chunk, chunk), lanes], jnp.max))

        peak = lax.fori_loop(1, 10, top, fold(acc[pl.ds(0, chunk), lanes], jnp.max))
        peak = jnp.max(peak, axis=0, keepdims=True)

        def add(i, sums):
            logits = acc[pl.ds(i * chunk, chunk), lanes]
            shifted = logits - peak
            weights = jnp.exp(shifted)
            place = lax.broadcasted_iota(jnp.int32, (chunk, 128), 0) + i * chunk
            hit = jnp.where(place == wanted, logits, 0.0)
            return (
                sums[0] + fold(weights, jnp.sum),
                sums[1] + fold(weights * shifted, jnp.sum),
                sums[2] + fold(hit, jnp.sum),
            )

        none = jnp.zeros((8, 128), F32)
        sums = lax.fori_loop(0, 10, add, (none, none, none))
        sums = [jnp.sum(s, axis=0, keepdims=True) for s in sums]
        stats[tile] = stack_rows(peak, *sums)
        return carry

    lax.fori_loop(0, NY, summarize, 0)

    def swap(stage, buffer, own, at, source=None):
        copies = []
        for d in range(1, 8):
            src = buffer.at[own] if source is None else source((own + d) % 8)
            copy = remote(src, buffer.at[own], t_s.at[stage, d - 1], t_r.at[stage, d - 1], at(d))
            copy.start()
            copies.append(copy)
        for copy in copies:
            copy.wait_recv()
        return copies

    done = []
    got_y[y] = stats[y]
    done += swap(0, got_y, y, at_y, lambda i: stats.at[i])
    got_c[mine] = stack_rows(*merge_tiles([got_y[i] for i in range(8)]))
    done += swap(1, got_c, mine, at_c)
    peak, total, spread, target = merge_tiles([got_c[i] for i in range(8)])

    kept = side_values(toks[y, :, NZ])[3:4]
    log_total = jnp.log(total)
    entropy = kept * (log_total - spread / total)
    logprob = kept * (target - peak - log_total)
    final[...] = stack_rows(entropy, logprob)

    lane = lax.broadcasted_iota(jnp.int32, (128, 128), 1)
    slot = lane // 16
    token = ((((y * NX + slot % NX) * NC + slot // NX) * NZ) + w) * 16 + lane % 16
    member = ((token >= bounds[0]) & (token < bounds[1])).astype(F32)
    sum_z[w] = lax.dot_general(
        stack_rows(logprob), member, NT, precision=lax.Precision.HIGHEST, preferred_element_type=F32
    )
    done += swap(2, sum_z, w, at_z)
    sum_y[y] = functools.reduce(jnp.add, [sum_z[i] for i in range(8)])
    done += swap(3, sum_y, y, at_y)
    seq[...] = functools.reduce(jnp.add, [sum_y[i] for i in range(8)])

    for copy in sent + xs + [cross] + done + list(yring.values()) + list(ring.values()):
        copy.wait_send()


def per_device(hidden, norm_gain, head_weight, targets, pad_mask, lengths):
    rows, wide = head_weight.shape
    packed = jnp.concatenate(
        [hidden.reshape(NZ, 16, wide), jnp.broadcast_to(norm_gain[None, None], (NZ, 16, wide))], axis=1
    )
    columns = jnp.stack([targets // 4096, (targets // 64) % 64, targets % 64, pad_mask], axis=1)
    digits = jnp.pad(columns.astype(jnp.bfloat16), ((0, 0), (0, wide - 4)))
    seq_ends = jnp.cumsum(lengths)
    bounds = jnp.pad(jnp.stack([seq_ends - lengths, seq_ends]), ((0, 0), (0, 128 - lengths.shape[0])))
    bounds = jnp.broadcast_to(bounds[:, :, None], (2, 128, 128))
    vmem = pl.BlockSpec(memory_space=pltpu.VMEM)
    dma = pltpu.SemaphoreType.DMA
    bf = jnp.bfloat16
    final, seq = pl.pallas_call(
        kernel,
        out_shape=(jax.ShapeDtypeStruct((8, 128), F32), jax.ShapeDtypeStruct((8, 128), F32)),
        in_specs=[vmem] * 4,
        out_specs=(vmem, vmem),
        scratch_shapes=[
            pltpu.VMEM((NZ, 32, wide), bf),
            pltpu.VMEM((NY, GROUP, NZ + 1, 16, wide), bf),
            pltpu.VMEM((NZ, rows, wide), bf),
            pltpu.VMEM((rows, 1024), F32),
            pltpu.VMEM((8, 8, 128), F32),
            pltpu.VMEM((8, 8, 128), F32),
            pltpu.VMEM((8, 8, 128), F32),
            pltpu.VMEM((8, 8, 128), F32),
            pltpu.VMEM((8, 8, 128), F32),
            dma((7,)), dma((7,)),
            dma((2, 7, 2)), dma((2, 7, 2)),
            dma((3,)), dma((3,)),
            dma((2, 4)), dma((2, 4)),
            dma((1,)), dma((1,)),
            dma((4, 7)), dma((4, 7)),
        ],
        compiler_params=pltpu.CompilerParams(
            collective_id=0, has_side_effects=True, vmem_limit_bytes=50 << 20
        ),
    )(packed, digits, head_weight, bounds)
    v = lax.axis_index("vocab")
    first = ((v % NC) * NX + (v // NC) % NX) * 16
    own = lax.dynamic_slice(final, (0, first), (2, 16))
    return (own[0], own[1], seq[0, : lengths.shape[0]] / lengths.astype(F32))


def solution(mesh):
    placed = (
        P("vocab", "width"),
        P("width"),
        P("vocab", "width"),
        P(("vocab", "width")),
        P(("vocab", "width")),
        P(),
    )
    return jax.shard_map(
        per_device,
        mesh=mesh,
        in_specs=placed,
        out_specs=(P(("vocab", "width")), P(("vocab", "width")), P()),
        check_vma=False,
    )
```

time: 491 us -> 112 us (0.23)
  blocking collectives: 302 us -> 0 us
  waiting for transfers between devices: 142 us -> 0 us
  Pallas kernels: 0 us -> 106 us
  between operations: 14.9 us -> 0.74 us
  matrix products: 12.9 us -> 0 us
  other arithmetic: 9.19 us -> 0.78 us
    all_gather x4 -> x0, blocking collectives: 154 us -> none  [merged_2(): pieces = jax.tree.map(lambda part: lax.all_gather(part, axis), value)]
    all_gather x2 -> x0, waiting for transfers between devices: 142 us -> none  [the longest x1 83.2 us: per_device(): head_full = lax.all_gather(head_weight, 'width', axis=1, tiled=True)]
    psum x2 -> x0, blocking collectives: 116 us -> none  [the longest x1 95.3 us: per_device(): lax.psum(partial_value, ('vocab', 'width')) / lengths.astype(jnp.float32)]
    pallas_call x0 -> x1, Pallas kernels: none -> 106 us  [per_device(): pl.pallas_call(kernel, out_shape=(jax.ShapeDtypeStruct((8, 128), F32), ja...]
    unnamed x1 -> x0, blocking collectives: 22.5 us -> none
    dot_general x2 -> x0, matrix products: 12.9 us -> none  [per_block(): lax.dot_general(inputs[0], head_full, contract, preferred_element_type=jn...]
    all_to_all x1 -> x0, blocking collectives: 9.6 us -> none  [per_device(): lax.all_to_all(normed, 'width', split_axis=0, concat_axis=1, tiled=True)]
  transfers between devices with their start and end apart: 2 -> 0, of which waited for: 2 -> 0; matrix products, arithmetic and copies ran while one was open for 1% -> 0% of each run, Pallas kernels for 0% -> 0%
where the time goes in v1:
time: 112 us
  Pallas kernels  106 us (95%)
  local copies, waits for them, and re-layouts  4.18 us (4%)
    pallas_call x1, Pallas kernels, per_device(): pl.pallas_call(kernel, out_shape=(jax.ShapeDtypeStruct((8, 128), F32), ja...  106 us
    unnamed x10, local copies, waits for them, and re-layouts  2.6 us

profile of v1, /device:TPU:1, one launch (start us, length us, event | category | flops | bytes accessed | tf_op | source)
XLA Modules:
  0.0 111.6 jit_solution(3397824953849442912)
XLA Ops:
  0.6 0.0 copy-start.1
  0.6 0.7 broadcast_in_dim.4
  1.3 0.1 copy-done.1
  1.5 0.0 copy-start.3
  1.5 0.0 copy-start.4
  1.5 0.6 copy-done.3
  2.1 0.0 copy-done.4
  2.2 0.1 copy.19
  2.3 0.0 copy-start.2
  2.3 0.7 copy-done.2
  2.9 0.1 copy.20
  3.0 0.1 reduce-window.4
  3.1 0.1 reduce
  3.3 0.1 broadcast_in_dim.5.bounds
  3.4 0.0 copy-start
  3.4 1.1 %copy-done = bf16[1600,256]{1,0:T(8,128)(2,1)S(1)} copy-done((bf16[1600,256]{1,0:T(8,128)(2,1)S(1)}, bf16[1600,256]{1,0:T(8,128)(2,1)}, u32[]{:S(2)}) %copy-start) | copy-done | bytes 819224
  4.5 105.9 %shard_map.85 = (f32[8,128]{1,0:T(8,128)S(1)}, f32[8,128]{1,0:T(8,128)S(1)}) custom-call(bf16[8,32,256]{2,1,0:T(8,128)(2,1)S(1)} %pad_maximum_fusion.packed, bf16[16,256]{1,0:T(8,128)(2,1)S(1)} %pad.8.digits, bf16[1600,256]{1,0:T(8,128)(2,1)S(1)} %copy-done, s32[2,128,128]{2,1,0:T(8,128)S(1)} %broadcast_in_dim.5.bounds), custom_call_target="tpu_custom_call" | custom-call | tf_op jit(solution)/shard_map/pallas_call | solution.py:270
  110.5 0.1 constant_dynamic-slice_fusion
  110.5 0.5 slice_bitcast_fusion
  111.1 0.5 bitcast_divide_fusion
  (7 shorter events, 0.1 us)
Async XLA Ops:
  0.6 0.8 copy-start.1
  1.5 0.7 copy-start.3
  1.5 0.7 copy-start.4
  2.3 0.7 copy-start.2
  3.4 1.2 %copy-start = (bf16[1600,256]{1,0:T(8,128)(2,1)S(1)}, bf16[1600,256]{1,0:T(8,128)(2,1)}, u32[]{:S(2)}) copy-start(bf16[1600,256]{1,0:T(8,128)(2,1)} %head.1) | copy-start | bytes 2457604

commit v2 on v1

--- a/solution.py
+++ b/solution.py
@@ -40,9 +40,9 @@
 
 
 def kernel(
-    packed, digits, head, bounds, final, seq,
-    raw, toks, heads, acc, stats, got_y, got_c, sum_z, sum_y,
-    az_s, az_r, h_s, h_r, x_s, x_r, y_s, y_r, c_s, c_r, t_s, t_r,
+    hidden, gain_row, digits, head, bounds, final, seq,
+    raw, gains, toks, heads, acc, wanted, run, stats, got_y, got_c, sum_z, sum_y,
+    az_s, az_r, g_s, g_r, h_s, h_r, x_s, x_r, y_s, y_r, c_s, c_r, t_s, t_r, own_s,
 ):
     v = lax.axis_index("vocab")
     w = lax.axis_index("width")
@@ -51,8 +51,9 @@
     y = v // (NC * NX)
     mine = core * NX + x
     rows, wide = head.shape
-    ways, parts = 2, 2
-    piece = rows // (ways * parts)
+    ways, parts = 2, 4
+    half = rows // ways
+    edges = [(half // 16 * i + parts - 1) // parts * 16 for i in range(parts)] + [half]
 
     def at_z(d):
         return {"width": (w + d) % NZ}
@@ -73,41 +74,60 @@
             pl.semaphore_signal(barrier, inc=1, device_id=device, device_id_type=MESH)
     pl.semaphore_wait(barrier, 21)
 
+    def rows_of(z):
+        return hidden.at[pl.ds(pl.multiple_of(z * 16, 16), 16)]
+
+    local = [
+        pltpu.make_async_copy(rows_of(w), raw.at[w], own_s.at[0]),
+        pltpu.make_async_copy(gain_row, gains.at[w], own_s.at[1]),
+        pltpu.make_async_copy(head, heads.at[w], own_s.at[2]),
+    ]
+    for copy in local:
+        copy.start()
     sent = []
     for d in range(1, NZ):
-        copy = remote(packed.at[(w + d) % NZ], raw.at[w], az_s.at[d - 1], az_r.at[d - 1], at_z(d))
+        to = (w + d) % NZ
+        sent.append(remote(rows_of(to), raw.at[w], az_s.at[d - 1], az_r.at[d - 1], at_z(d)))
+        sent.append(remote(gain_row, gains.at[w], g_s.at[d - 1], g_r.at[d - 1], at_z(d)))
+    for copy in sent:
         copy.start()
-        sent.append(copy)
-
-    def head_copy(step, way, part):
-        span = pl.ds((way * parts + part) * piece, piece)
-        owner = (w - step + NZ) % NZ if way == 0 else (w + step) % NZ
-        src = head.at[span] if step == 0 else heads.at[owner, span]
-        return remote(
-            src, heads.at[owner, span], h_s.at[way, step, part], h_r.at[way, step, part],
-            at_z(1 if way == 0 else NZ - 1),
-        )
 
     ring = {}
+
+    def head_arrive(step, part):
+        for way in range(ways):
+            ring[step - 1, way, part].wait_recv()
+
+    def rows_at(way, part):
+        return way * half + edges[part], edges[part + 1] - edges[part]
 
     def head_step(step):
         for part in range(parts):
             for way in range(ways):
                 if step > 0:
                     ring[step - 1, way, part].wait_recv()
-                if step < NZ - 1:
-                    copy = head_copy(step, way, part)
-                    copy.start()
-                    ring[step, way, part] = copy
+                span = pl.ds(*rows_at(way, part))
+                owner = (w - step + NZ) % NZ if way == 0 else (w + step) % NZ
+                slab = heads.at[owner, span]
+                copy = remote(
+                    head.at[span] if step == 0 else slab,
+                    slab,
+                    h_s.at[way, step, part],
+                    h_r.at[way, step, part],
+                    at_z(1 if way == 0 else NZ - 1),
+                )
+                copy.start()
+                ring[step, way, part] = copy
 
     head_step(0)
-    raw[w] = packed[w]
     acc[...] = jnp.zeros_like(acc)
+    for copy in local:
+        copy.wait()
     for copy in sent:
         copy.wait_recv()
 
-    values = raw[:, 0:16, :].astype(F32)
-    gain = raw[:, 16:32, :].astype(F32)
+    values = raw[...].astype(F32)
+    gain = gains[...].astype(F32)
     energy = jnp.sum(jnp.sum(values * values, axis=0), axis=1, keepdims=True)
     inv = lax.rsqrt(energy / (wide * NZ) + epsilon)
     toks[y, mine, 0:NZ] = (values * inv[None] * gain).astype(jnp.bfloat16)
@@ -145,9 +165,7 @@
     cross = remote(side, side, c_s.at[0], c_r.at[0], {"vocab": v - core + (1 - core)})
     cross.start()
 
-    half = rows // ways
-
-    def multiply(near, far):
+    def multiply(near, far, spans):
         def one(i, carry):
             step = near + i // 4
             tile = i % 4
@@ -155,23 +173,14 @@
             for way in range(ways):
                 owner = (w - step + NZ) % NZ if way == 0 else (w + step) % NZ
                 tokens = toks[pl.ds(tile * 2, 2), :, owner].reshape(256, wide)
-                block = heads[owner, pl.ds(way * half, half)]
-                span = pl.ds(way * half, half)
-                acc[span, lanes] += lax.dot_general(block, tokens, NT, preferred_element_type=F32)
+                span = pl.ds(*spans[way])
+                acc[span, lanes] += lax.dot_general(
+                    heads[owner, span], tokens, NT, preferred_element_type=F32
+                )
             return carry
 
         lax.fori_loop(0, (far - near) * 4, one, 0)
 
-    heads[w] = head[...]
-    head_step(5)
-    cross.wait_recv()
-    multiply(0, 3)
-    head_step(6)
-    multiply(3, 7)
-    head_step(7)
-    multiply(7, 8)
-
-    chunk = rows // 10
     pick = (
         lax.broadcasted_iota(jnp.int32, (8, 256), 0) == lax.broadcasted_iota(jnp.int32, (8, 256), 1)
     ).astype(jnp.bfloat16)
@@ -179,40 +188,74 @@
     def side_values(block):
         return lax.dot_general(pick, block.reshape(128, 256), NT, preferred_element_type=F32)
 
-    def fold(values, op):
-        return op(values.reshape(chunk // 8, 8, 128), axis=0)
-
-    def summarize(tile, carry):
-        lanes = pl.ds(pl.multiple_of(tile * 128, 128), 128)
+    def note_wanted(tile, carry):
         extra = side_values(toks[tile, :, NZ])
-        wanted = extra[0:1] * 4096.0 + extra[1:2] * 64.0 + extra[2:3] - (v * rows).astype(F32)
-        wanted = wanted.astype(jnp.int32)
-
-        def top(i, peak):
-            return jnp.maximum(peak, fold(acc[pl.ds(i * chunk, chunk), lanes], jnp.max))
-
-        peak = lax.fori_loop(1, 10, top, fold(acc[pl.ds(0, chunk), lanes], jnp.max))
-        peak = jnp.max(peak, axis=0, keepdims=True)
-
-        def add(i, sums):
-            logits = acc[pl.ds(i * chunk, chunk), lanes]
-            shifted = logits - peak
-            weights = jnp.exp(shifted)
-            place = lax.broadcasted_iota(jnp.int32, (chunk, 128), 0) + i * chunk
-            hit = jnp.where(place == wanted, logits, 0.0)
-            return (
-                sums[0] + fold(weights, jnp.sum),
-                sums[1] + fold(weights * shifted, jnp.sum),
-                sums[2] + fold(hit, jnp.sum),
-            )
-
-        none = jnp.zeros((8, 128), F32)
-        sums = lax.fori_loop(0, 10, add, (none, none, none))
-        sums = [jnp.sum(s, axis=0, keepdims=True) for s in sums]
-        stats[tile] = stack_rows(peak, *sums)
+        index = extra[0:1] * 4096.0 + extra[1:2] * 64.0 + extra[2:3] - (v * rows).astype(F32)
+        wanted[tile] = jnp.broadcast_to(index, (8, 128)).astype(jnp.int32)
         return carry
 
-    lax.fori_loop(0, NY, summarize, 0)
+    def summarize(part):
+        def one(tile, carry):
+            lanes = pl.ds(pl.multiple_of(tile * 128, 128), 128)
+            chunks = []
+            for way in range(ways):
+                base, count = rows_at(way, part)
+                chunks += [(base + i * (count // 2), count // 2) for i in range(2)]
+
+            def block(base, count):
+                return acc[pl.ds(base, count), lanes].reshape(count // 8, 8, 128)
+
+            peak = functools.reduce(jnp.maximum, [jnp.max(block(*c), axis=0) for c in chunks])
+            target = wanted[tile] - lax.broadcasted_iota(jnp.int32, (8, 128), 0)
+            sums = [jnp.zeros((8, 128), F32)] * 3
+            if part > 0:
+                before = run[tile, 0]
+                peak = jnp.maximum(before, peak)
+                gap = before - peak
+                lift = jnp.exp(gap)
+                sums = [
+                    run[tile, 1] * lift,
+                    lift * (run[tile, 2] + gap * run[tile, 1]),
+                    run[tile, 3],
+                ]
+            for base, count in chunks:
+                logits = block(base, count)
+                shifted = logits - peak[None]
+                weights = jnp.exp(shifted)
+                place = lax.broadcasted_iota(jnp.int32, logits.shape, 0) * 8 + base
+                hit = jnp.where(place == target[None], logits, 0.0)
+                sums = [
+                    sums[0] + jnp.sum(weights, axis=0),
+                    sums[1] + jnp.sum(weights * shifted, axis=0),
+                    sums[2] + jnp.sum(hit, axis=0),
+                ]
+            run[tile, 0] = peak
+            for k in range(3):
+                run[tile, k + 1] = sums[k]
+            return carry
+
+        lax.fori_loop(0, NY, one, 0)
+
+    def close():
+        for tile in range(NY):
+            peak = jnp.max(run[tile, 0], axis=0, keepdims=True)
+            gap = run[tile, 0] - peak
+            lift = jnp.exp(gap)
+            rest = (run[tile, 1] * lift, lift * (run[tile, 2] + gap * run[tile, 1]), run[tile, 3])
+            stats[tile] = stack_rows(peak, *[jnp.sum(t, axis=0, keepdims=True) for t in rest])
+
+    whole = [(way * half, half) for way in range(ways)]
+    head_step(5)
+    cross.wait_recv()
+    lax.fori_loop(0, NY, note_wanted, 0)
+    multiply(0, 3, whole)
+    head_step(6)
+    multiply(3, 7, whole)
+    for part in range(parts):
+        head_arrive(7, part)
+        multiply(7, 8, [rows_at(way, part) for way in range(ways)])
+        summarize(part)
+    close()
 
     def swap(stage, buffer, own, at, source=None):
         copies = []
@@ -256,43 +299,46 @@
 
 def per_device(hidden, norm_gain, head_weight, targets, pad_mask, lengths):
     rows, wide = head_weight.shape
-    packed = jnp.concatenate(
-        [hidden.reshape(NZ, 16, wide), jnp.broadcast_to(norm_gain[None, None], (NZ, 16, wide))], axis=1
-    )
     columns = jnp.stack([targets // 4096, (targets // 64) % 64, targets % 64, pad_mask], axis=1)
     digits = jnp.pad(columns.astype(jnp.bfloat16), ((0, 0), (0, wide - 4)))
     seq_ends = jnp.cumsum(lengths)
     bounds = jnp.pad(jnp.stack([seq_ends - lengths, seq_ends]), ((0, 0), (0, 128 - lengths.shape[0])))
     bounds = jnp.broadcast_to(bounds[:, :, None], (2, 128, 128))
     vmem = pl.BlockSpec(memory_space=pltpu.VMEM)
+    hbm = pl.BlockSpec(memory_space=pl.ANY)
     dma = pltpu.SemaphoreType.DMA
     bf = jnp.bfloat16
     final, seq = pl.pallas_call(
         kernel,
         out_shape=(jax.ShapeDtypeStruct((8, 128), F32), jax.ShapeDtypeStruct((8, 128), F32)),
-        in_specs=[vmem] * 4,
+        in_specs=[hbm, hbm, vmem, hbm, vmem],
         out_specs=(vmem, vmem),
         scratch_shapes=[
-            pltpu.VMEM((NZ, 32, wide), bf),
+            pltpu.VMEM((NZ, 16, wide), bf),
+            pltpu.VMEM((NZ, 1, wide), bf),
             pltpu.VMEM((NY, GROUP, NZ + 1, 16, wide), bf),
             pltpu.VMEM((NZ, rows, wide), bf),
             pltpu.VMEM((rows, 1024), F32),
+            pltpu.VMEM((NY, 8, 128), jnp.int32),
+            pltpu.VMEM((NY, 4, 8, 128), F32),
             pltpu.VMEM((8, 8, 128), F32),
             pltpu.VMEM((8, 8, 128), F32),
             pltpu.VMEM((8, 8, 128), F32),
             pltpu.VMEM((8, 8, 128), F32),
             pltpu.VMEM((8, 8, 128), F32),
             dma((7,)), dma((7,)),
-            dma((2, 7, 2)), dma((2, 7, 2)),
+            dma((7,)), dma((7,)),
+            dma((2, 7, 4)), dma((2, 7, 4)),
             dma((3,)), dma((3,)),
             dma((2, 4)), dma((2, 4)),
             dma((1,)), dma((1,)),
             dma((4, 7)), dma((4, 7)),
+            dma((3,)),
         ],
         compiler_params=pltpu.CompilerParams(
             collective_id=0, has_side_effects=True, vmem_limit_bytes=50 << 20
         ),
-    )(packed, digits, head_weight, bounds)
+    )(hidden, norm_gain[None], digits, head_weight, bounds)
     v = lax.axis_index("vocab")
     first = ((v % NC) * NX + (v // NC) % NX) * 16
     own = lax.dynamic_slice(final, (0, first), (2, 16))

time: 112 us -> 111 us (level)
    pallas_call x1, Pallas kernels: 106 us -> 105 us  [per_device(): pl.pallas_call(kernel, out_shape=(jax.ShapeDtypeStruct((8, 128), F32), ja...]
where the time goes in v2:
time: 111 us; the launch traced here: 110 us
  Pallas kernels  105 us (95%)
  local copies, waits for them, and re-layouts  4.11 us (4%)
    pallas_call x1, Pallas kernels, per_device(): pl.pallas_call(kernel, out_shape=(jax.ShapeDtypeStruct((8, 128), F32), ja...  105 us
    unnamed x10, local copies, waits for them, and re-layouts  2.55 us

profile of v2, /device:TPU:1, one launch (start us, length us, event | category | flops | bytes accessed | tf_op | source)
XLA Modules:
  0.0 110.3 jit_solution(3843355190687508104)
XLA Ops:
  0.6 0.0 copy-start.3
  0.6 0.0 copy-start.4
  0.7 0.7 broadcast_in_dim.4.gain_row
  1.3 0.0 copy-done.3
  1.3 0.0 copy-done.4
  1.4 0.1 copy.19
  1.5 0.0 copy-start.2
  1.5 0.7 copy-done.2
  2.1 0.1 copy.20
  2.2 0.1 reduce-window.4
  2.3 0.1 reduce
  2.5 0.0 copy-start.1
  2.5 0.1 broadcast_in_dim.10.bounds
  2.6 0.7 copy-done.1
  3.3 0.0 copy-start
  3.3 1.1 %copy-done = bf16[1600,256]{1,0:T(8,128)(2,1)S(1)} copy-done((bf16[1600,256]{1,0:T(8,128)(2,1)S(1)}, bf16[1600,256]{1,0:T(8,128)(2,1)}, u32[]{:S(2)}) %copy-start) | copy-done | bytes 819224
  4.5 104.7 %shard_map.85 = (f32[8,128]{1,0:T(8,128)S(1)}, f32[8,128]{1,0:T(8,128)S(1)}) custom-call(bf16[128,256]{1,0:T(8,128)(2,1)S(1)} %copy-done.1, bf16[1,256]{1,0:T(2,128)(2,1)S(1)} %broadcast_in_dim.4.gain_row, bf16[16,256]{1,0:T(8,128)(2,1)S(1)} %pad.8.digits, bf16[1600,256]{1,0:T(8,128)(2,1)S(1)} %copy-done, s32[2,128,128]{2,1,0:T(8,128)S(1)} %broadcast_in_dim.10.bounds), custom_call_target="tpu_custom_call" | custom-call | tf_op jit(solution)/shard_map/pallas_call | solution.py:311
  109.2 0.1 constant_dynamic-slice_fusion
  109.2 0.5 slice_bitcast_fusion
  109.8 0.5 bitcast_divide_fusion
  (6 shorter events, 0.1 us)
Async XLA Ops:
  0.6 0.7 copy-start.3
  0.6 0.7 copy-start.4
  1.5 0.7 copy-start.2
  2.5 0.8 copy-start.1
  3.3 1.1 %copy-start = (bf16[1600,256]{1,0:T(8,128)(2,1)S(1)}, bf16[1600,256]{1,0:T(8,128)(2,1)}, u32[]{:S(2)}) copy-start(bf16[1600,256]{1,0:T(8,128)(2,1)} %head.1) | copy-start | bytes 2457604

commit v3 on v2

--- a/solution.py
+++ b/solution.py
@@ -139,10 +139,19 @@
         copy = remote(spot, spot, x_s.at[d - 1], x_r.at[d - 1], at_x(d))
         copy.start()
         xs.append(copy)
+    head_step(1)
     for copy in xs:
         copy.wait_recv()
 
     yring = {}
+    cross = []
+
+    def cross_block(owner):
+        block = toks.at[owner, pl.ds(core * NX, NX)]
+        k = len(cross)
+        copy = remote(block, block, c_s.at[k], c_r.at[k], {"vocab": v - core + (1 - core)})
+        copy.start()
+        cross.append(copy)
 
     def y_step(step):
         for way, hops in ((0, NY // 2), (1, NY // 2 - 1)):
@@ -156,15 +165,13 @@
                 )
                 copy.start()
                 yring[step, way] = copy
+            if step <= hops and (step > 0 or way == 0):
+                cross_block((y - step + NY) % NY if way == 0 else (y + step) % NY)
 
     y_step(0)
     for step in range(1, NY // 2 + 1):
-        head_step(step)
+        head_step(step + 1)
         y_step(step)
-    side = toks.at[:, pl.ds(core * NX, NX)]
-    cross = remote(side, side, c_s.at[0], c_r.at[0], {"vocab": v - core + (1 - core)})
-    cross.start()
-
     def multiply(near, far, spans):
         def one(i, carry):
             step = near + i // 4
@@ -245,8 +252,8 @@
             stats[tile] = stack_rows(peak, *[jnp.sum(t, axis=0, keepdims=True) for t in rest])
 
     whole = [(way * half, half) for way in range(ways)]
-    head_step(5)
-    cross.wait_recv()
+    for copy in cross:
+        copy.wait_recv()
     lax.fori_loop(0, NY, note_wanted, 0)
     multiply(0, 3, whole)
     head_step(6)
@@ -293,7 +300,7 @@
     done += swap(3, sum_y, y, at_y)
     seq[...] = functools.reduce(jnp.add, [sum_y[i] for i in range(8)])
 
-    for copy in sent + xs + [cross] + done + list(yring.values()) + list(ring.values()):
+    for copy in sent + xs + cross + done + list(yring.values()) + list(ring.values()):
         copy.wait_send()
 
 
@@ -331,7 +338,7 @@
             dma((2, 7, 4)), dma((2, 7, 4)),
             dma((3,)), dma((3,)),
             dma((2, 4)), dma((2, 4)),
-            dma((1,)), dma((1,)),
+            dma((8,)), dma((8,)),
             dma((4, 7)), dma((4, 7)),
             dma((3,)),
         ],

time: 111 us -> 110 us (level)
  no operation moved by 1% of the time
where the time goes in v3:
time: 110 us; the launch traced here: 109 us
  Pallas kernels  104 us (95%)
  local copies, waits for them, and re-layouts  4.11 us (4%)
    pallas_call x1, Pallas kernels, per_device(): pl.pallas_call(kernel, out_shape=(jax.ShapeDtypeStruct((8, 128), F32), ja...  104 us
    unnamed x10, local copies, waits for them, and re-layouts  2.55 us

profile of v3, /device:TPU:1, one launch (start us, length us, event | category | flops | bytes accessed | tf_op | source)
XLA Modules:
  0.0 109.4 jit_solution(14472040168104305486)
XLA Ops:
  0.6 0.0 copy-start.3
  0.6 0.0 copy-start.4
  0.7 0.7 broadcast_in_dim.4.gain_row
  1.3 0.0 copy-done.3
  1.3 0.0 copy-done.4
  1.4 0.1 copy.19
  1.5 0.0 copy-start.2
  1.5 0.7 copy-done.2
  2.1 0.1 copy.20
  2.2 0.1 reduce-window.4
  2.3 0.1 reduce
  2.5 0.0 copy-start.1
  2.5 0.1 broadcast_in_dim.10.bounds
  2.6 0.7 copy-done.1
  3.3 0.0 copy-start
  3.3 1.1 %copy-done = bf16[1600,256]{1,0:T(8,128)(2,1)S(1)} copy-done((bf16[1600,256]{1,0:T(8,128)(2,1)S(1)}, bf16[1600,256]{1,0:T(8,128)(2,1)}, u32[]{:S(2)}) %copy-start) | copy-done | bytes 819224
  4.5 103.8 %shard_map.85 = (f32[8,128]{1,0:T(8,128)S(1)}, f32[8,128]{1,0:T(8,128)S(1)}) custom-call(bf16[128,256]{1,0:T(8,128)(2,1)S(1)} %copy-done.1, bf16[1,256]{1,0:T(2,128)(2,1)S(1)} %broadcast_in_dim.4.gain_row, bf16[16,256]{1,0:T(8,128)(2,1)S(1)} %pad.8.digits, bf16[1600,256]{1,0:T(8,128)(2,1)S(1)} %copy-done, s32[2,128,128]{2,1,0:T(8,128)S(1)} %broadcast_in_dim.10.bounds), custom_call_target="tpu_custom_call" | custom-call | tf_op jit(solution)/shard_map/pallas_call | solution.py:318
  108.3 0.1 constant_dynamic-slice_fusion
  108.4 0.5 slice_bitcast_fusion
  108.9 0.5 bitcast_divide_fusion
  (6 shorter events, 0.1 us)
Async XLA Ops:
  0.6 0.7 copy-start.3
  0.6 0.7 copy-start.4
  1.5 0.7 copy-start.2
  2.5 0.8 copy-start.1
  3.3 1.1 %copy-start = (bf16[1600,256]{1,0:T(8,128)(2,1)S(1)}, bf16[1600,256]{1,0:T(8,128)(2,1)}, u32[]{:S(2)}) copy-start(bf16[1600,256]{1,0:T(8,128)(2,1)} %head.1) | copy-start | bytes 2457604
